TPU v7x, 32 devices: a whole 2x2x4 slice. The times are simulated.
32 devices in a mesh: row: 4 (over x, core), col: 8 (over z, y).
Axes of the slice: x: 2, y: 2, z: 4, core: 2. Of those that a mesh axis runs over, the one named last changes fastest.
Arguments:
- points: bfloat16 [12, 4, 512, 64], P(None, 'row', 'col'), may hold values from -7.5 to 7.5
- inverse_factor: bfloat16 [512, 512], replicated, as said below
- panel_index: int32 [1], replicated, may hold values from 3 to 23
- column_map: int32 [8], P('col'), may hold values from 0 to 7, each once
Outputs:
- panel: bfloat16 [6, 4, 512, 512], P(None, 'row', 'col')
- update: bfloat16 [6, 4, 512, 8, 512], P(None, 'row', None, 'col')
Inputs may be any that keep to these rules, and one draw needn't show every extreme that they name: `column_map`: a permutation of 0 .. 8 - 1. `inverse_factor`: zero above the diagonal.
All inputs are finite; a program needn't handle non-finite values.
Results may differ from a plain program's by a relative error of at most 0.0049.
Values may be sent and summed in bfloat16 or wider, within the bound.
No kernel may reach another device: no remote copies, remote signals or barrier semaphores. Data moves between devices by JAX's collectives and lax.ppermute only.
A program may use at most 64 MiB of HBM per device.

v0:
```python
import jax
import jax.numpy as jnp
from jax import lax
from jax.sharding import PartitionSpec as P

RW = 6
JITTER = 1.0


def kernel_tile(left_points, right_points):
    left_vals = left_points.astype(jnp.float32)
    right_vals = right_points.astype(jnp.float32)
    inner_products = lax.dot_general(
        left_points, right_points, (((1,), (1,)), ((), ())), preferred_element_type=jnp.float32
    )
    left_norms = jnp.sum(left_vals * left_vals, axis=1)
    right_norms = jnp.sum(right_vals * right_vals, axis=1)
    distance = left_norms[:, None] + right_norms[None, :] - 2.0 * inner_products
    return jnp.exp(-distance / (2.0 * left_points.shape[1]))


def panel_tile(row_points, panel_points, inverse_factor):
    rounded = kernel_tile(row_points, panel_points).astype(jnp.bfloat16)
    product = lax.dot_general(
        rounded, inverse_factor, (((1,), (1,)), ((), ())), preferred_element_type=jnp.float32
    )
    return product.astype(jnp.bfloat16)


def masked(values, keep):
    return jnp.where(keep, values.astype(jnp.float32), 0.0)


def shards(points, inverse_factor, panel_index, column_map):
    row_count = lax.axis_size("row")
    row_here = lax.axis_index("row")
    col_here = lax.axis_index("col")
    pivot_tile = panel_index[0]
    start_slot = (pivot_tile + row_count - row_here) // row_count
    local_points = lax.dynamic_slice_in_dim(points[:, 0], start_slot - 1, RW + 1, 0)
    blocks = lax.all_gather(local_points, "col", axis=1, tiled=True)
    holds_panel = row_here == pivot_tile % row_count
    panel_points = lax.psum(masked(blocks[0], holds_panel).astype(jnp.bfloat16), "row")
    window_points = blocks[1:]
    panel_full = jnp.stack(
        [
            panel_tile(window_points[window_slot], panel_points, inverse_factor)
            for window_slot in range(RW)
        ]
    )
    share_rows = local_points.shape[1]
    panel_part = lax.dynamic_slice_in_dim(panel_full, col_here * share_rows, share_rows, 1)
    column_tile = pivot_tile + 1 + column_map[0]
    holds_column = row_here == column_tile % row_count
    position = jnp.clip(column_tile // row_count - start_slot, 0, RW - 1)
    candidate_points = lax.dynamic_index_in_dim(window_points, position, 0, keepdims=False)
    candidate_rows = lax.dynamic_index_in_dim(panel_full, position, 0, keepdims=False)
    summed_points, summed_rows = (
        lax.psum(masked(candidate_points, holds_column).astype(jnp.bfloat16), "row").astype(
            jnp.float32
        ),
        lax.psum(masked(candidate_rows, holds_column).astype(jnp.bfloat16), "row").astype(
            jnp.float32
        ),
    )
    column_points = summed_points.astype(jnp.bfloat16)
    column_rows = summed_rows.astype(jnp.bfloat16)
    identity = jnp.eye(inverse_factor.shape[0], dtype=jnp.float32)
    updates = []
    for window_slot in range(RW):
        tile_row = (start_slot + window_slot) * row_count + row_here
        update_tile = kernel_tile(window_points[window_slot], column_points)
        update_tile = update_tile + jnp.where(tile_row == column_tile, JITTER, 0.0) * identity
        update_tile = update_tile - lax.dot_general(
            panel_full[window_slot],
            column_rows,
            (((1,), (1,)), ((), ())),
            preferred_element_type=jnp.float32,
        )
        updates.append(update_tile.astype(jnp.bfloat16))
    update = jnp.stack(updates)[:, None, :, None, :]
    return (panel_part[:, None], update)


def solution(mesh):
    in_specs = (P(None, "row", "col", None), P(), P(), P("col"))
    out_specs = (P(None, "row", "col", None), P(None, "row", None, "col", None))
    return jax.shard_map(shards, mesh=mesh, in_specs=in_specs, out_specs=out_specs, check_vma=False)
```

profile of v0, /device:TPU:0, one launch (start us, length us, event | category | flops | bytes accessed | tf_op | source)
XLA Modules:
  0.0 141.9 jit_solution(7604250753707338826)
XLA Ops:
  7.2 0.0 copy-start
  7.2 0.0 all-reduce.4.cloned.1.call-start
  8.0 0.9 constant_dynamic-slice_fusion
  8.9 34.2 %all-gather = bf16[7,1,512,64]{3,2,1,0:T(8,128)(2,1)S(1)} all-gather(bf16[7,1,64,64]{3,2,1,0:T(8,128)(2,1)S(1)} %constant_dynamic-slice_fusion), channel_id=2, replica_groups=mesh['row'=4,'col'=8] {'col'}, dimensions={2}, use_global_device_ids=true | all-gather | bytes 516096 | tf_op jit(solution)/shard_map/all_gather | solution.py:41
  43.1 0.7 fusion.109
  43.8 0.0 all-reduce.4.cloned.1.call-update
  43.8 0.0 all-reduce.6.cloned.1.call-start
  43.9 0.5 multiply_reduce_fusion.1
  44.4 0.0 copy-start.7
  44.4 0.0 copy-start.8
  44.4 0.1 slice.59
  45.1 0.7 fusion.110
  45.8 30.7 %all-reduce.4.cloned.1.call-done = bf16[512,64]{1,0:T(8,128)(2,1)} async-done(((bf16[512,64]{1,0:T(8,128)(2,1)}), bf16[512,64]{1,0:T(8,128)(2,1)}) %all-reduce.4.cloned.1.call-update) | async-done | bytes 65552 | tf_op jit(solution)/shard_map/psum | solution.py:43
  76.6 1.1 multiply_reduce_fusion.6
  77.7 0.0 copy-start.9
  77.7 0.0 copy-done
  77.7 2.5 %bitcast_dynamic-update-slice_fusion.5 = (bf16[6,512,512]{2,1,0:T(8,128)(2,1)}, bf16[512,512]{1,0:T(8,128)(2,1)}) fusion(bf16[512,512]{1,0:T(8,128)(2,1)S(1)} %copy-done, bf16[512,64]{1,0:T(8,128)(2,1)} %all-reduce.4.cloned.1.call-done, f32[512]{0:T(512)S(1)} %multiply_reduce_fusion.6, f32[512]{0:T(512)S(1)} %get-tuple-element.9, ...), kind=kOutput, calls=%fused_computation.116 | convolution fusion | flops 303824896 | bytes 1773568 | tf_op jit(solution)/shard_map/dot_general | solution.py:24
  80.2 0.0 copy-done.5
  80.2 1.6 %bitcast_dynamic-update-slice_fusion.4 = (bf16[6,512,512]{2,1,0:T(8,128)(2,1)}, bf16[512,512]{1,0:T(8,128)(2,1)}) fusion(bf16[6,512,512]{2,1,0:T(8,128)(2,1)} %get-tuple-element.12, bf16[512,512]{1,0:T(8,128)(2,1)S(1)} %copy-done, bf16[512,64]{1,0:T(8,128)(2,1)S(1)} %copy-done.5, f32[512]{0:T(512)S(1)} %get-tuple-element.8, ...), kind=kOutput, calls=%fused_computation.115 | convolution fusion | flops 303824896 | bytes 1839104 | tf_op jit(solution)/shard_map/dot_general | solution.py:24
  81.9 0.0 copy-done.7
  81.9 1.4 %bitcast_dynamic-update-slice_fusion.3 = (bf16[6,512,512]{2,1,0:T(8,128)(2,1)}, bf16[512,512]{1,0:T(8,128)(2,1)S(1)}) fusion(bf16[6,512,512]{2,1,0:T(8,128)(2,1)} %get-tuple-element.14, bf16[512,512]{1,0:T(8,128)(2,1)S(1)} %copy-done, bf16[512,64]{1,0:T(8,128)(2,1)S(1)} %copy-done.5, f32[512]{0:T(512)S(1)} %get-tuple-element.7, ...), kind=kOutput, calls=%fused_computation.114 | convolution fusion | flops 303824896 | bytes 1839104 | tf_op jit(solution)/shard_map/dot_general | solution.py:24
  83.3 1.4 %bitcast_dynamic-update-slice_fusion.2 = (bf16[6,512,512]{2,1,0:T(8,128)(2,1)}, bf16[512,512]{1,0:T(8,128)(2,1)S(1)}) fusion(bf16[6,512,512]{2,1,0:T(8,128)(2,1)} %get-tuple-element.16, bf16[512,512]{1,0:T(8,128)(2,1)S(1)} %copy-done, bf16[512,64]{1,0:T(8,128)(2,1)S(1)} %copy-done.5, f32[512]{0:T(512)S(1)} %get-tuple-element.6, ...), kind=kOutput, calls=%fused_computation.113 | convolution fusion | flops 303824896 | bytes 1839104 | tf_op jit(solution)/shard_map/dot_general | solution.py:24
  84.8 1.4 %bitcast_dynamic-update-slice_fusion.1 = (bf16[6,512,512]{2,1,0:T(8,128)(2,1)}, bf16[512,512]{1,0:T(8,128)(2,1)S(1)}) fusion(bf16[6,512,512]{2,1,0:T(8,128)(2,1)} %get-tuple-element.18, bf16[512,512]{1,0:T(8,128)(2,1)S(1)} %copy-done, bf16[512,64]{1,0:T(8,128)(2,1)S(1)} %copy-done.5, f32[512]{0:T(512)S(1)} %get-tuple-element.5, ...), kind=kOutput, calls=%fused_computation.112 | convolution fusion | flops 303824896 | bytes 1839104 | tf_op jit(solution)/shard_map/dot_general | solution.py:24
  86.2 2.3 %bitcast_dynamic-update-slice_fusion = (bf16[6,512,512]{2,1,0:T(8,128)(2,1)}, bf16[512,512]{1,0:T(8,128)(2,1)S(1)}) fusion(bf16[6,512,512]{2,1,0:T(8,128)(2,1)} %get-tuple-element.20, bf16[512,512]{1,0:T(8,128)(2,1)S(1)} %copy-done, bf16[512,64]{1,0:T(8,128)(2,1)} %all-reduce.4.cloned.1.call-done, f32[512]{0:T(512)S(1)} %get-tuple-element.4, ...), kind=kOutput, calls=%fused_computation.111 | convolution fusion | flops 303824896 | bytes 1839104 | tf_op jit(solution)/shard_map/dot_general | solution.py:24
  88.5 1.9 %fusion.84 = bf16[512,512]{1,0:T(8,128)(2,1)} fusion(bf16[6,512,512]{2,1,0:T(8,128)(2,1)} %get-tuple-element.22, s32[]{:T(128)S(6)} %min.4, pred[]{:T(512)S(6)} %eq.41), kind=kLoop, calls=%fused_computation.110 | loop fusion | flops 786432 | bytes 1048581 | tf_op jit(solution)/shard_map/convert_element_type | solution.py:62
  90.5 0.0 all-reduce.6.cloned.1.call-update
  90.6 1.8 %dynamic-slice_bitcast_fusion = bf16[6,1,64,512]{3,2,1,0:T(8,128)(2,1)} fusion(bf16[6,512,512]{2,1,0:T(8,128)(2,1)} %get-tuple-element.22, s32[]{:T(128)S(6)} %select_n.77), kind=kLoop, calls=%fused_computation.141 | loop fusion | bytes 786436 | tf_op jit(solution)/shard_map/broadcast_in_dim | solution.py:82
  92.3 32.4 %all-reduce.6.cloned.1.call-done = (bf16[512,64]{1,0:T(8,128)(2,1)}, bf16[512,512]{1,0:T(8,128)(2,1)}) async-done(((bf16[512,64]{1,0:T(8,128)(2,1)}, bf16[512,512]{1,0:T(8,128)(2,1)}), (bf16[512,64]{1,0:T(8,128)(2,1)}, bf16[512,512]{1,0:T(8,128)(2,1)})) %all-reduce.6.cloned.1.call-update) | async-done | bytes 589840 | tf_op jit(solution)/shard_map/psum | solution.py:59
  124.8 1.1 multiply_reduce_fusion
  125.9 1.3 fusion.28
  127.2 1.3 fusion.33
  128.5 0.0 copy-done.4
  128.5 0.4 fusion.38
  128.9 0.4 fusion.43
  129.4 0.0 copy-start.1
  129.4 0.0 copy-start.3
  129.4 0.4 fusion.48
  129.8 0.4 fusion.53
  130.2 0.2 copy-done.1
  130.4 0.2 copy-done.3
  130.6 0.5 fusion.77
  131.0 0.5 fusion.75
  131.5 0.5 fusion.73
  132.0 0.5 fusion.71
  132.5 0.5 fusion.69
  133.0 0.5 fusion.67
  133.4 0.0 copy-start.6
  133.4 1.7 %copy-done.6 = bf16[6,512,512]{2,1,0:T(8,128)(2,1)} copy-done((bf16[6,512,512]{2,1,0:T(8,128)(2,1)}, bf16[6,512,512]{2,1,0:T(8,128)(2,1)S(1)}, u32[]{:S(2)}) %copy-start.6) | copy-done | bytes 3145752
  (6 shorter events, 0.0 us)
Async XLA Ops:
  7.2 70.5 %copy-start = (bf16[512,512]{1,0:T(8,128)(2,1)S(1)}, bf16[512,512]{1,0:T(8,128)(2,1)}, u32[]{:S(2)}) copy-start(bf16[512,512]{1,0:T(8,128)(2,1)} %param.5) | copy-start | bytes 1572868
  7.2 69.4 %all-reduce.4.cloned.1.call-start = ((), (), s32[]{:S(2)}) async-start(), calls=%async_computation | async-start | bytes 262144 | tf_op jit(solution)/shard_map/psum | solution.py:43
  43.8 80.9 %all-reduce.6.cloned.1.call-start = ((), (), s32[]{:S(2)}) async-start(), calls=%async_computation.1 | async-start | bytes 1310720 | tf_op jit(solution)/shard_map/psum | solution.py:59
  44.4 37.5 %copy-start.7 = (f32[512]{0:T(512)}, f32[512]{0:T(512)S(1)}, u32[]{:S(2)}) copy-start(f32[512]{0:T(512)S(1)} %get-tuple-element.8) | copy-start | bytes 6148
  44.4 37.5 %copy-start.8 = (f32[512]{0:T(512)}, f32[512]{0:T(512)S(1)}, u32[]{:S(2)}) copy-start(f32[512]{0:T(512)S(1)} %get-tuple-element.9) | copy-start | bytes 6148
  76.6 3.7 %copy-start.5 = (bf16[512,64]{1,0:T(8,128)(2,1)S(1)}, bf16[512,64]{1,0:T(8,128)(2,1)}, u32[]{:S(2)}) copy-start(bf16[512,64]{1,0:T(8,128)(2,1)} %all-reduce.4.cloned.1.call-done) | copy-start | bytes 196612
  77.7 7.1 %copy-start.9 = (f32[512]{0:T(512)}, f32[512]{0:T(512)S(1)}, u32[]{:S(2)}) copy-start(f32[512]{0:T(512)S(1)} %multiply_reduce_fusion.6) | copy-start | bytes 6148
  124.8 3.8 %copy-start.4 = (bf16[512,64]{1,0:T(8,128)(2,1)S(1)}, bf16[512,64]{1,0:T(8,128)(2,1)}, u32[]{:S(2)}) copy-start(bf16[512,64]{1,0:T(8,128)(2,1)} %get-tuple-element.10) | copy-start | bytes 196612
  129.4 1.0 copy-start.1
  129.4 1.2 copy-start.3
  129.8 1.3 copy-start.2
  133.4 1.7 %copy-start.6 = (bf16[6,512,512]{2,1,0:T(8,128)(2,1)}, bf16[6,512,512]{2,1,0:T(8,128)(2,1)S(1)}, u32[]{:S(2)}) copy-start(bf16[6,512,512]{2,1,0:T(8,128)(2,1)S(1)} %fusion.67) | copy-start | bytes 9437188
Sparse Core Ops, SparseCore 0:
  43.9 32.5 all-reduce.3
  90.6 34.0 all-reduce.5
where the time goes:
time: 142 us
  waiting for transfers between devices  63.2 us (45%)
  blocking collectives  34.2 us (24%)
  matrix products  17.8 us (13%)
  between operations  15.7 us (11%)
  other arithmetic  6.04 us (4%)
  local copies, waits for them, and re-layouts  4.81 us (3%)
    all_gather x1, blocking collectives, shards(): blocks = lax.all_gather(local_points, 'col', axis=1, tiled=True)  34.2 us
    psum x1, waiting for transfers between devices, shards(): lax.psum(masked(candidate_points, holds_column).astype(jnp.bfloat16), 'row')  32.4 us
    psum x1, waiting for transfers between devices, shards(): lax.psum(masked(blocks[0], holds_panel).astype(jnp.bfloat16), 'row')  30.7 us
    dot_general x6, matrix products, panel_tile(): lax.dot_general(rounded, inverse_factor, (((1,), (1,)), ((), ())), prefer...  10.8 us
    dot_general x6, matrix products, kernel_tile(): lax.dot_general(left_points, right_points, (((1,), (1,)), ((), ())), pref...  4.21 us
  transfers between devices with their start and end apart: 2, of which 2 were waited for; matrix products, arithmetic and copies ran while one was open for 2% of the time, Pallas kernels for 0%

commit v1 on v0

--- a/solution.py
+++ b/solution.py
@@ -40,7 +40,9 @@
     local_points = lax.dynamic_slice_in_dim(points[:, 0], start_slot - 1, RW + 1, 0)
     blocks = lax.all_gather(local_points, "col", axis=1, tiled=True)
     holds_panel = row_here == pivot_tile % row_count
-    panel_points = lax.psum(masked(blocks[0], holds_panel).astype(jnp.bfloat16), "row")
+    panel_points = jnp.sum(
+        lax.all_gather(masked(blocks[0], holds_panel).astype(jnp.bfloat16), "row"), axis=0
+    )
     window_points = blocks[1:]
     panel_full = jnp.stack(
         [

time: 142 us -> 121 us (0.85)
  waiting for transfers between devices: 63.2 us -> 33 us
  blocking collectives: 34.2 us -> 40.4 us
  local copies, waits for them, and re-layouts: 4.81 us -> 8.8 us
    psum x1 -> x0, waiting for transfers between devices: 30.7 us -> none  [shards(): lax.psum(masked(blocks[0], holds_panel).astype(jnp.bfloat16), 'row')]
    all_gather x0 -> x1, blocking collectives: none -> 5.78 us  [shards(): lax.all_gather(masked(blocks[0], holds_panel).astype(jnp.bfloat16), 'row')]
    unnamed x20 -> x33, local copies, waits for them, and re-layouts: 2.06 us -> 4.2 us
  transfers between devices with their start and end apart: 2 -> 1, of which waited for: 2 -> 1; matrix products, arithmetic and copies ran while one was open for 2% -> 1% of each run, Pallas kernels for 0% -> 0%
where the time goes in v1:
time: 121 us
  blocking collectives  40.4 us (33%)
  waiting for transfers between devices  33 us (27%)
  matrix products  17.7 us (15%)
  between operations  15.8 us (13%)
  local copies, waits for them, and re-layouts  8.8 us (7%)
  other arithmetic  5.21 us (4%)
    all_gather x1, blocking collectives, shards(): blocks = lax.all_gather(local_points, 'col', axis=1, tiled=True)  34.6 us
    psum x1, waiting for transfers between devices, shards(): lax.psum(masked(candidate_points, holds_column).astype(jnp.bfloat16), 'row')  33 us
    dot_general x6, matrix products, panel_tile(): lax.dot_general(rounded, inverse_factor, (((1,), (1,)), ((), ())), prefer...  10.6 us
    all_gather x1, blocking collectives, shards(): lax.all_gather(masked(blocks[0], holds_panel).astype(jnp.bfloat16), 'row')  5.78 us
    dot_general x6, matrix products, kernel_tile(): lax.dot_general(left_points, right_points, (((1,), (1,)), ((), ())), pref...  4.25 us
    unnamed x33, local copies, waits for them, and re-layouts  4.2 us
    dot_general x6, matrix products, shards(): lax.dot_general(panel_full[window_slot], column_rows, (((1,), (1,)), ((),...  2.82 us
  transfers between devices with their start and end apart: 1, of which 1 were waited for; matrix products, arithmetic and copies ran while one was open for 1% of the time, Pallas kernels for 0%

profile of v1, /device:TPU:0, one launch (start us, length us, event | category | flops | bytes accessed | tf_op | source)
XLA Modules:
  0.0 120.9 jit_solution(6632456020772741132)
XLA Ops:
  7.2 0.0 copy-start
  7.2 0.0 all-reduce.3.cloned.1.call-start
  8.0 0.9 constant_dynamic-slice_fusion.1
  8.9 0.1 copy.22
  9.0 34.6 %all-gather = bf16[7,1,512,64]{3,0,1,2:T(8,128)(2,1)S(1)} all-gather(bf16[7,1,64,64]{3,0,1,2:T(8,128)(2,1)S(1)} %copy.22), channel_id=2, replica_groups=mesh['row'=4,'col'=8] {'col'}, dimensions={2}, use_global_device_ids=true | all-gather | bytes 516096 | tf_op jit(solution)/shard_map/all_gather | solution.py:41
  43.6 1.4 %fusion.141 = (bf16[1,1,512,64]{3,0,1,2:T(2,128)(2,1)S(1)}, bf16[1,1,512,64]{3,0,1,2:T(2,128)(2,1)S(1)}, bf16[1,1,512,64]{3,0,1,2:T(2,128)(2,1)S(1)}, bf16[1,1,5...) fusion(bf16[7,1,512,64]{3,0,1,2:T(8,128)(2,1)S(1)} %all-gather), kind=kLoop, calls=%fused_computation.180 | loop fusion | bytes 917504 | tf_op jit(solution)/shard_map/slice | solution.py:49
  44.9 0.3 slice.59
  45.9 0.1 copy.24
  46.0 5.8 %all_gather.8 = bf16[4,512,64]{1,2,0:T(8,128)(2,1)S(1)} all-gather(bf16[1,512,64]{1,2,0:T(8,128)(2,1)S(1)} %fusion.109), channel_id=1, replica_groups=mesh['row'=4,'col'=8] {'row'}, dimensions={0}, use_global_device_ids=true | all-gather | bytes 327680 | tf_op jit(solution)/shard_map/all_gather | solution.py:44
  51.9 0.0 copy-start.3
  51.9 0.6 copy-done.3
  52.5 0.1 copy.23
  52.7 0.1 copy.25
  52.8 0.6 multiply_reduce_fusion.5
  53.4 0.1 copy.26
  53.5 0.1 copy.27
  53.7 0.1 copy.28
  53.9 0.1 copy.29
  54.0 0.3 constant_dynamic-slice_fusion
  54.3 0.7 copy.31
  55.1 1.6 %bitcast_dynamic-update-slice_fusion.5 = (bf16[6,512,512]{2,1,0:T(8,128)(2,1)}, bf16[512,512]{1,0:T(8,128)(2,1)}) fusion(bf16[512,512]{1,0:T(8,128)(2,1)S(1)} %copy-done, bf16[512,64]{0,1:T(8,128)(2,1)S(1)} %copy-done.4, f32[512]{0:T(512)S(1)} %multiply_reduce_fusion.6, f32[512]{0:T(512)S(1)} %multiply_reduce_fusion.7, bf16[1,1,512,64]{2,3,1,0:T(8,128)(2,1)S(1)} %copy.23), kind=kOutput, calls=%fused_computation.116 | convolution fusion | flops 303824896 | bytes 1708032 | tf_op jit(solution)/shard_map/dot_general | solution.py:24
  56.7 2.3 %bitcast_dynamic-update-slice_fusion.4 = (bf16[6,512,512]{2,1,0:T(8,128)(2,1)}, bf16[512,512]{1,0:T(8,128)(2,1)S(1)}) fusion(bf16[6,512,512]{2,1,0:T(8,128)(2,1)} %get-tuple-element.19, bf16[512,512]{1,0:T(8,128)(2,1)S(1)} %copy-done, bf16[512,64]{0,1:T(8,128)(2,1)} %copy-done.3, f32[512]{0:T(512)S(1)} %copy-done.8, f32[512]{0:T(512)} %copy-done.10, ...), kind=kOutput, calls=%fused_computation.115 | convolution fusion | flops 303824896 | bytes 1708032 | tf_op jit(solution)/shard_map/dot_general | solution.py:24
  59.0 1.5 %bitcast_dynamic-update-slice_fusion.3 = (bf16[6,512,512]{2,1,0:T(8,128)(2,1)}, bf16[512,512]{1,0:T(8,128)(2,1)S(1)}) fusion(bf16[6,512,512]{2,1,0:T(8,128)(2,1)} %get-tuple-element.21, bf16[512,512]{1,0:T(8,128)(2,1)S(1)} %copy-done, bf16[512,64]{0,1:T(8,128)(2,1)S(1)} %copy-done.5, f32[512]{0:T(512)S(1)} %multiply_reduce_fusion.4, ...), kind=kOutput, calls=%fused_computation.114 | convolution fusion | flops 303824896 | bytes 1708032 | tf_op jit(solution)/shard_map/dot_general | solution.py:24
  60.5 1.5 %bitcast_dynamic-update-slice_fusion.2 = (bf16[6,512,512]{2,1,0:T(8,128)(2,1)}, bf16[512,512]{1,0:T(8,128)(2,1)S(1)}) fusion(bf16[6,512,512]{2,1,0:T(8,128)(2,1)} %get-tuple-element.23, bf16[512,512]{1,0:T(8,128)(2,1)S(1)} %copy-done, bf16[512,64]{0,1:T(8,128)(2,1)S(1)} %copy-done.5, f32[512]{0:T(512)S(1)} %multiply_reduce_fusion.3, ...), kind=kOutput, calls=%fused_computation.113 | convolution fusion | flops 303824896 | bytes 1708032 | tf_op jit(solution)/shard_map/dot_general | solution.py:24
  61.9 1.5 %bitcast_dynamic-update-slice_fusion.1 = (bf16[6,512,512]{2,1,0:T(8,128)(2,1)}, bf16[512,512]{1,0:T(8,128)(2,1)S(1)}) fusion(bf16[6,512,512]{2,1,0:T(8,128)(2,1)} %get-tuple-element.25, bf16[512,512]{1,0:T(8,128)(2,1)S(1)} %copy-done, bf16[512,64]{0,1:T(8,128)(2,1)S(1)} %copy-done.5, f32[512]{0:T(512)S(1)} %multiply_reduce_fusion.2, ...), kind=kOutput, calls=%fused_computation.112 | convolution fusion | flops 303824896 | bytes 1708032 | tf_op jit(solution)/shard_map/dot_general | solution.py:24
  63.4 2.3 %bitcast_dynamic-update-slice_fusion = (bf16[6,512,512]{2,1,0:T(8,128)(2,1)}, bf16[512,512]{1,0:T(8,128)(2,1)S(1)}) fusion(bf16[6,512,512]{2,1,0:T(8,128)(2,1)} %get-tuple-element.27, bf16[512,512]{1,0:T(8,128)(2,1)S(1)} %copy-done, bf16[512,64]{0,1:T(8,128)(2,1)} %copy-done.3, f32[512]{0:T(512)S(1)} %multiply_reduce_fusion.1, f32[512]{0:T(512)} %copy-done.10, ...), kind=kOutput, calls=%fused_computation.111 | convolution fusion | flops 303824896 | bytes 1708032 | tf_op jit(solution)/shard_map/dot_general | solution.py:24
  65.7 1.5 %fusion.110 = bf16[512,64]{0,1:T(8,128)(2,1)} fusion(bf16[1,1,512,64]{2,3,1,0:T(8,128)(2,1)} %copy.31, pred[]{:T(512)S(6)} %eq.41), kind=kLoop, calls=%fused_computation.153 | loop fusion | flops 98304 | bytes 131073 | tf_op jit(solution)/shard_map/convert_element_type | solution.py:61
  67.2 1.9 %fusion.84 = bf16[512,512]{1,0:T(8,128)(2,1)} fusion(bf16[6,512,512]{2,1,0:T(8,128)(2,1)} %get-tuple-element.29, s32[]{:T(128)S(6)} %min.4, pred[]{:T(512)S(6)} %eq.41), kind=kLoop, calls=%fused_computation.110 | loop fusion | flops 786432 | bytes 1048581 | tf_op jit(solution)/shard_map/convert_element_type | solution.py:64
  69.1 0.0 all-reduce.3.cloned.1.call-update
  69.2 1.8 %dynamic-slice_bitcast_fusion = bf16[6,1,64,512]{3,2,1,0:T(8,128)(2,1)} fusion(bf16[6,512,512]{2,1,0:T(8,128)(2,1)} %get-tuple-element.29, s32[]{:T(128)S(6)} %select_n.77), kind=kLoop, calls=%fused_computation.141 | loop fusion | bytes 786436 | tf_op jit(solution)/shard_map/broadcast_in_dim | solution.py:84
  71.0 33.0 %all-reduce.3.cloned.1.call-done = (bf16[512,64]{0,1:T(8,128)(2,1)}, bf16[512,512]{1,0:T(8,128)(2,1)}) async-done(((bf16[512,64]{0,1:T(8,128)(2,1)}, bf16[512,512]{1,0:T(8,128)(2,1)}), (bf16[512,64]{0,1:T(8,128)(2,1)}, bf16[512,512]{1,0:T(8,128)(2,1)})) %all-reduce.3.cloned.1.call-update) | async-done | bytes 589840 | tf_op jit(solution)/shard_map/psum | solution.py:61
  103.9 0.9 multiply_reduce_fusion
  104.9 1.3 %fusion.38 = f32[512,512]{1,0:T(8,128)S(1)} fusion(bf16[512,64]{0,1:T(8,128)(2,1)} %get-tuple-element.10, f32[]{:T(128)S(6)} %select_n.82, f32[512]{0:T(512)S(1)} %multiply_reduce_fusion, f32[512]{0:T(512)} %copy-done.9, bf16[1,1,512,64]{2,3,1,0:T(8,128)(2,1)S(1)} %copy.23), kind=kOutput, calls=%fused_computation.56 | convolution fusion | flops 35651584 | bytes 1183748 | tf_op jit(solution)/shard_map/dot_general | solution.py:13
  106.2 1.3 %fusion.41 = f32[512,512]{1,0:T(8,128)S(1)} fusion(bf16[512,64]{0,1:T(8,128)(2,1)} %get-tuple-element.10, f32[]{:T(128)S(6)} %select_n.85, f32[512]{0:T(512)S(1)} %multiply_reduce_fusion, f32[512]{0:T(512)} %multiply_reduce_fusion.5, bf16[1,1,512,64]{2,3,1,0:T(8,128)(2,1)S(1)} %copy.25), kind=kOutput, calls=%fused_computation.59 | convolution fusion | flops 35651584 | bytes 1183748 | tf_op jit(solution)/shard_map/dot_general | solution.py:13
  107.4 0.4 fusion.44
  107.9 0.4 fusion.47
  108.3 0.4 fusion.50
  108.8 0.4 fusion.53
  109.2 0.2 copy-done.1
  109.4 0.2 copy-done.2
  109.5 0.5 fusion.77
  110.0 0.5 fusion.75
  110.5 0.5 fusion.73
  110.9 0.5 fusion.71
  111.4 0.5 fusion.69
  111.9 0.5 fusion.67
  112.4 0.0 copy-start.6
  112.4 1.7 %copy-done.6 = bf16[6,512,512]{2,1,0:T(8,128)(2,1)} copy-done((bf16[6,512,512]{2,1,0:T(8,128)(2,1)}, bf16[6,512,512]{2,1,0:T(8,128)(2,1)S(1)}, u32[]{:S(2)}) %copy-start.6) | copy-done | bytes 3145752
  (25 shorter events, 0.3 us)
Async XLA Ops:
  7.2 47.9 %copy-start = (bf16[512,512]{1,0:T(8,128)(2,1)S(1)}, bf16[512,512]{1,0:T(8,128)(2,1)}, u32[]{:S(2)}) copy-start(bf16[512,512]{1,0:T(8,128)(2,1)} %param.5) | copy-start | bytes 1572868
  7.2 96.8 %all-reduce.3.cloned.1.call-start = ((), (), s32[]{:S(2)}) async-start(), calls=%async_computation | async-start | bytes 1179648 | tf_op jit(solution)/shard_map/psum | solution.py:61
  51.9 0.6 copy-start.3
  52.5 4.2 %copy-start.10 = (f32[512]{0:T(512)}, f32[512]{0:T(512)S(1)}, u32[]{:S(2)}) copy-start(f32[512]{0:T(512)S(1)} %multiply_reduce_fusion.6) | copy-start | bytes 6148
  52.5 2.6 %copy-start.4 = (bf16[512,64]{0,1:T(8,128)(2,1)S(1)}, bf16[512,64]{0,1:T(8,128)(2,1)}, u32[]{:S(2)}) copy-start(bf16[512,64]{0,1:T(8,128)(2,1)} %copy-done.3) | copy-start | bytes 196612
  52.6 4.1 %copy-start.9 = (f32[512]{0:T(512)}, f32[512]{0:T(512)S(1)}, u32[]{:S(2)}) copy-start(f32[512]{0:T(512)S(1)} %multiply_reduce_fusion.7) | copy-start | bytes 6148
  53.5 3.2 %copy-start.8 = (f32[512]{0:T(512)S(1)}, f32[512]{0:T(512)}, u32[]{:S(2)}) copy-start(f32[512]{0:T(512)} %multiply_reduce_fusion.5) | copy-start | bytes 6148
  55.1 4.0 %copy-start.5 = (bf16[512,64]{0,1:T(8,128)(2,1)S(1)}, bf16[512,64]{0,1:T(8,128)(2,1)}, u32[]{:S(2)}) copy-start(bf16[512,64]{0,1:T(8,128)(2,1)} %copy-done.3) | copy-start | bytes 196612
  56.7 2.3 %copy-start.11 = (f32[512]{0:T(512)S(1)}, f32[512]{0:T(512)}, u32[]{:S(2)}) copy-start(f32[512]{0:T(512)} %copy-done.10) | copy-start | bytes 6148
  103.9 3.5 %copy-start.7 = (bf16[512,64]{0,1:T(8,128)(2,1)S(1)}, bf16[512,64]{0,1:T(8,128)(2,1)}, u32[]{:S(2)}) copy-start(bf16[512,64]{0,1:T(8,128)(2,1)} %get-tuple-element.10) | copy-start | bytes 196612
  108.3 1.0 copy-start.1
  108.3 1.2 copy-start.2
  112.4 1.7 %copy-start.6 = (bf16[6,512,512]{2,1,0:T(8,128)(2,1)}, bf16[6,512,512]{2,1,0:T(8,128)(2,1)S(1)}, u32[]{:S(2)}) copy-start(bf16[6,512,512]{2,1,0:T(8,128)(2,1)S(1)} %fusion.67) | copy-start | bytes 9437188
Sparse Core Ops, SparseCore 0:
  69.3 34.6 all-reduce.2
